TPU v7x, 32 devices: a whole 2x2x4 slice. The times are simulated.
32 devices in a mesh: probe: 4 (over z), gx: 4 (over x, core), gy: 2 (over y).
Axes of the slice: x: 2, y: 2, z: 4, core: 2. Of those that a mesh axis runs over, the one named last changes fastest.
Arguments:
- wave_prev: float32 [4, 128, 256, 256], P('probe', 'gx', 'gy'), may hold values from -6 to 6
- wave_cur: float32 [4, 128, 256, 256], P('probe', 'gx', 'gy'), may hold values from -6 to 6
- courant: float32 [128, 256, 256], P('gx', 'gy'), may hold values from 0.02 to 0.16
- perturb: float32 [4, 128, 256, 256], P('probe', 'gx', 'gy'), may hold values from -4 to 4
- snapshots: bfloat16 [8, 128, 256, 256], P('probe', 'gx', 'gy'), may hold values from -6 to 6
- step_slots: int32 [6], replicated, may hold values from 0 to 7, as said below
- precond: float32 [256], replicated, may hold values from 0.5 to 2
- probe_ids: int32 [4], P('probe'), may hold values from 0 to 255, as said below
Outputs:
- earlier: float32 [4, 128, 256, 256], P('probe', 'gx', 'gy')
- latest: float32 [4, 128, 256, 256], P('probe', 'gx', 'gy')
Inputs may be any that keep to these rules, and one draw needn't show every extreme that they name: `step_slots`: distinct slots; 0 and 7 are always among them. `probe_ids`: distinct indices; 0 and 255 are always among them.
All inputs are finite; a program needn't handle non-finite values.
Results may differ from a plain program's by a relative error of at most 0.0003.
Values may be sent and summed in bfloat16 or wider, within the bound.
A program may use at most 192 MiB of HBM per device.

v0:
```python
import jax
import jax.numpy as jnp
from jax import lax
from jax.sharding import PartitionSpec as P

STEPS = 4


COEFFS = (-205.0 / 72.0, 8.0 / 5.0, -1.0 / 5.0, 8.0 / 315.0, -1.0 / 560.0)


def spread(value, axis, source):
    kept = jnp.where(lax.axis_index(axis) == source, value, 0).astype(value.dtype)
    return lax.psum(kept, axis)


def with_halo(block, sides, width):
    for axis, dim in sides:
        count = lax.axis_size(axis)
        forward = [(i, i + 1) for i in range(count - 1)]
        backward = [(target, source) for source, target in forward]
        low = lax.ppermute(
            lax.slice_in_dim(block, block.shape[dim] - width, None, axis=dim), axis, forward
        )
        high = lax.ppermute(lax.slice_in_dim(block, 0, width, axis=dim), axis, backward)
        block = jnp.concatenate([low, block, high], axis=dim)
    return block


def stencil(padded, field):
    extent_x = field.shape[1]
    extent_y = field.shape[2]
    extent_z = field.shape[3]
    total = 3.0 * COEFFS[0] * field
    for offset in range(1, 5):
        factor = COEFFS[offset]
        along = padded[:, 4 + offset : 4 + offset + extent_x, 4 : 4 + extent_y, 4 : 4 + extent_z]
        along = (
            along
            + padded[:, 4 - offset : 4 - offset + extent_x, 4 : 4 + extent_y, 4 : 4 + extent_z]
        )
        along = (
            along
            + padded[:, 4 : 4 + extent_x, 4 + offset : 4 + offset + extent_y, 4 : 4 + extent_z]
        )
        along = (
            along
            + padded[:, 4 : 4 + extent_x, 4 - offset : 4 - offset + extent_y, 4 : 4 + extent_z]
        )
        along = (
            along
            + padded[:, 4 : 4 + extent_x, 4 : 4 + extent_y, 4 + offset : 4 + offset + extent_z]
        )
        along = (
            along
            + padded[:, 4 : 4 + extent_x, 4 : 4 + extent_y, 4 - offset : 4 - offset + extent_z]
        )
        total = total + factor * along
    return total


def shards(wave_prev, wave_cur, courant, perturb, snapshots, step_slots, precond, probe_ids):
    table = jnp.arange(precond.shape[0], dtype=jnp.int32)
    matches = (probe_ids[:, None] == table[None, :]).astype(jnp.float32)
    weight = jnp.sum(matches * precond[None, :], axis=1)
    scaled = weight[:, None, None, None] * perturb
    slot_dev = snapshots.shape[0]

    def fetch(position):
        wanted = step_slots[position]
        owner = wanted // slot_dev
        holding = lax.dynamic_index_in_dim(snapshots, wanted % slot_dev, 0, keepdims=False)
        return spread(holding, "probe", owner).astype(jnp.float32)

    frames = [fetch(0), fetch(1)]
    previous = wave_prev
    current = wave_cur
    for index in range(STEPS):
        frames.append(fetch(index + 2))
        source = frames[index + 2] - 2.0 * frames[index + 1] + frames[index]
        widened = with_halo(current, (("gx", 1), ("gy", 2)), 4)
        padded = jnp.pad(widened, ((0, 0), (0, 0), (0, 0), (4, 4)))
        laplace = stencil(padded, current)
        following = 2.0 * current - previous + courant[None] * laplace - scaled * source[None]
        previous = current
        current = following
    return (previous, current)


def solution(mesh):
    placed = (
        P("probe", "gx", "gy", None),
        P("probe", "gx", "gy", None),
        P("gx", "gy", None),
        P("probe", "gx", "gy", None),
        P("probe", "gx", "gy", None),
        P(),
        P(),
        P("probe"),
    )
    return jax.shard_map(
        shards,
        mesh=mesh,
        in_specs=placed,
        out_specs=(P("probe", "gx", "gy", None), P("probe", "gx", "gy", None)),
        check_vma=False,
    )
```

profile of v0, /device:TPU:0, one launch (start us, length us, event | category | flops | bytes accessed | tf_op | source)
XLA Modules:
  0.0 825.9 jit_solution(7365499890127130381)
XLA Ops:
  7.2 1.5 fusion.147
  23.9 9.4 %select_bitcast_fusion = (bf16[32,128,256]{2,1,0:T(8,128)(2,1)}, bf16[32,128,256]{2,1,0:T(8,128)(2,1)}, bf16[32,128,256]{2,1,0:T(8,128)(2,1)}, bf16[32,128,256]{...) fusion(bf16[2,32,128,256]{3,2,1,0:T(8,128)(2,1)} %param.12, s32[]{:T(128)S(6)} %select_n.154, ...), kind=kLoop, calls=%fused_computation.247 | loop fusion | flops 6291456 | bytes 25165854 | tf_op jit(solution)/shard_map/jit(_where)/select_n | solution.py:13
  34.6 2.4 collective-permute-start.1
  39.3 7.1 constant_dynamic-update-slice_fusion.1
  48.6 4.7 collective-permute-start.3
  56.2 5.8 select_maximum_fusion.12
  61.9 403.7 %all-reduce.7.cloned.1.call-done = (bf16[32,128,256]{2,1,0:T(8,128)(2,1)}, bf16[32,128,256]{2,1,0:T(8,128)(2,1)}, bf16[32,128,256]{2,1,0:T(8,128)(2,1)}, bf16[32...) async-done(((bf16[32,128,256]{2,1,0:T(8,128)(2,1)}, bf16[32,128,256]{2,1,0:T(8,128)(2,1)}, bf16[32,128,256]{2,1,0:T(8,128)(2,1)}, ...) | async-done | bytes 12582928 | tf_op jit(solution)/shard_map/psum | solution.py:14
  465.6 55.3 %fusion.103 = f32[1,32,128,256]{3,2,1,0:T(8,128)S(1)} fusion(f32[1,40,128,256]{3,2,1,0:T(8,128)} %copy-done.3, bf16[32,128,256]{2,1,0:T(8,128)(2,1)} %get-tuple-element.2, bf16[32,128,256]{2,1,0:T(8,128)(2,1)} %get-tuple-element.3, f32[1,40,4,256]{3,2,1,0:T(4,128)S(1)} %collective-permute-done.3, f32[1,40,4,256]{3,2,1,0:T(4,128)S(1)} %collective-permute-done.2, ...), kind=kLoop, calls=%fused_computation.183 | loop fusion | flops 52428800 | bytes 99942400 | tf_op jit(solution)/shard_map/sub | solution.py:84
  522.3 3.1 collective-permute-start.5
  525.4 1.5 collective-permute-done.5
  528.2 4.7 collective-permute-start.7
  535.6 4.9 pad_maximum_fusion
  540.5 8.7 %select_maximum_fusion.8 = f32[1,40,136,264]{3,2,1,0:T(8,128)} fusion(f32[1,40,4,256]{3,2,1,0:T(4,128)S(1)} %collective-permute-done.6, f32[1,40,4,256]{3,2,1,0:T(4,128)S(1)} %collective-permute-done.7, f32[1,4,128,256]{3,2,1,0:T(8,128)S(1)} %collective-permute-done.4, f32[1,32,128,256]{3,2,1,0:T(8,128)S(1)} %fusion.103, ...), kind=kLoop, calls=%fused_computation.16 | loop fusion | flops 17233920 | bytes 11315200 | tf_op jit(solution)/shard_map/concatenate | solution.py:26
  549.2 66.3 %fusion.74 = f32[1,32,128,256]{3,2,1,0:T(8,128)} fusion(f32[1,32,128,256]{3,2,1,0:T(8,128)} %copy-done, bf16[32,128,256]{2,1,0:T(8,128)(2,1)} %get-tuple-element.2, bf16[32,128,256]{2,1,0:T(8,128)(2,1)S(1)} %copy-done.4, bf16[32,128,256]{2,1,0:T(8,128)(2,1)} %get-tuple-element.5, f32[1,4,128,256]{3,2,1,0:T(8,128)S(1)} %collective-permute-done.5, ...), kind=kLoop, calls=%fused_computation.154 | loop fusion | flops 52428800 | bytes 95420416 | tf_op jit(solution)/shard_map/sub | solution.py:84
  618.3 7.1 collective-permute-start.9
  629.3 4.8 collective-permute-start.11
  636.7 4.9 pad_maximum_fusion.1
  641.6 8.7 %select_maximum_fusion.4 = f32[1,40,136,264]{3,2,1,0:T(8,128)} fusion(f32[1,40,4,256]{3,2,1,0:T(4,128)S(1)} %collective-permute-done.10, f32[1,40,4,256]{3,2,1,0:T(4,128)S(1)} %collective-permute-done.11, f32[1,4,128,256]{3,2,1,0:T(8,128)S(1)} %collective-permute-done.8, f32[1,32,128,256]{3,2,1,0:T(8,128)S(1)} %copy-done.1, ...), kind=kLoop, calls=%fused_computation.12 | loop fusion | flops 17233920 | bytes 11315200 | tf_op jit(solution)/shard_map/concatenate | solution.py:26
  650.3 65.8 %fusion.43 = f32[1,32,128,256]{3,2,1,0:T(8,128)} fusion(f32[1,32,128,256]{3,2,1,0:T(8,128)} %fusion.74, bf16[32,128,256]{2,1,0:T(8,128)(2,1)S(1)} %copy-done.4, bf16[32,128,256]{2,1,0:T(8,128)(2,1)} %get-tuple-element.6, bf16[32,128,256]{2,1,0:T(8,128)(2,1)} %get-tuple-element.5, f32[1,4,128,256]{3,2,1,0:T(8,128)S(1)} %collective-permute-done.9, ...), kind=kLoop, calls=%fused_computation.123 | loop fusion | flops 52428800 | bytes 95420416 | tf_op jit(solution)/shard_map/sub | solution.py:84
  718.9 9.8 %collective-permute-start.13 = (f32[1,4,128,256]{3,2,1,0:T(8,128)S(1)}, f32[1,4,128,256]{3,2,1,0:T(8,128)S(1)}, u32[]{:S(2)}, u32[]{:S(2)}) collective-permute-start(f32[1,4,128,256]{3,2,1,0:T(8,128)S(1)} %get-tuple-element.23), channel_id=1, source_target_pairs={{0,2},{2,4},{4,6},{1,3},{3,5},{5,7},{8,10},{10,12},{12,14},{9,11},... | collective-permute-start | bytes 1572872 | tf_op jit(solution)/shard_map/ppermute | solution.py:22
  732.6 4.8 collective-permute-start.15
  740.0 4.9 pad_maximum_fusion.2
  744.9 8.7 %select_maximum_fusion = f32[1,40,136,264]{3,2,1,0:T(8,128)} fusion(f32[1,40,4,256]{3,2,1,0:T(4,128)S(1)} %collective-permute-done.14, f32[1,40,4,256]{3,2,1,0:T(4,128)S(1)} %collective-permute-done.15, f32[1,4,128,256]{3,2,1,0:T(8,128)S(1)} %collective-permute-done.12, f32[1,32,128,256]{3,2,1,0:T(8,128)S(1)} %copy-done.2, ...), kind=kLoop, calls=%fused_computation.8 | loop fusion | flops 17233920 | bytes 11315200 | tf_op jit(solution)/shard_map/concatenate | solution.py:26
  753.5 65.5 %fusion.12 = f32[1,32,128,256]{3,2,1,0:T(8,128)} fusion(f32[1,32,128,256]{3,2,1,0:T(8,128)} %fusion.43, bf16[32,128,256]{2,1,0:T(8,128)(2,1)S(1)} %copy-done.5, bf16[32,128,256]{2,1,0:T(8,128)(2,1)} %get-tuple-element.6, f32[1,4,128,256]{3,2,1,0:T(8,128)S(1)} %collective-permute-done.13, f32[1,4,128,256]{3,2,1,0:T(8,128)S(1)} %collective-permute-done.12, ...), kind=kLoop, calls=%fused_computation.92 | loop fusion | flops 52428800 | bytes 95420416 | tf_op jit(solution)/shard_map/sub | solution.py:84
  (50 shorter events, 32.0 us)
Async XLA Ops:
  7.2 458.5 %all-reduce.7.cloned.1.call-start = ((), (), s32[]{:S(2)}) async-start(), calls=%async_computation | async-start | bytes 25165824 | tf_op jit(solution)/shard_map/psum | solution.py:14
  34.6 3.9 collective-permute-start.1
  37.0 9.4 %collective-permute-start = (f32[1,4,128,256]{3,2,1,0:T(8,128)S(1)}, f32[1,4,128,256]{3,2,1,0:T(8,128)S(1)}, u32[]{:S(2)}, u32[]{:S(2)}) collective-permute-start(f32[1,4,128,256]{3,2,1,0:T(8,128)S(1)} %get-tuple-element.37), channel_id=1, source_target_pairs={{2,0},{4,2},{6,4},{3,1},{5,3},{7,5},{10,8},{12,10},{14,12},{11,9},... | collective-permute-start | bytes 1572872 | tf_op jit(solution)/shard_map/ppermute | solution.py:25
  39.3 14.7 %copy-start.6 = (f32[256]{0:T(256)S(1)}, f32[256]{0:T(256)}, u32[]{:S(2)}) copy-start(f32[256]{0:T(256)} %param.14) | copy-start | bytes 3076
  47.3 8.9 %copy-start.3 = (f32[1,40,128,256]{3,2,1,0:T(8,128)}, f32[1,40,128,256]{3,2,1,0:T(8,128)S(1)}, u32[]{:S(2)}) copy-start(f32[1,40,128,256]{3,2,1,0:T(8,128)S(1)} %get-tuple-element.40) | copy-start | bytes 15728644
  47.3 7.4 collective-permute-start.2
  48.6 7.5 collective-permute-start.3
  520.9 19.6 %copy-start = (f32[1,32,128,256]{3,2,1,0:T(8,128)}, f32[1,32,128,256]{3,2,1,0:T(8,128)S(1)}, u32[]{:S(2)}) copy-start(f32[1,32,128,256]{3,2,1,0:T(8,128)S(1)} %fusion.103) | copy-start | bytes 12582916
  521.0 4.4 collective-permute-start.4
  522.3 4.6 collective-permute-start.5
  526.9 7.2 collective-permute-start.6
  528.2 7.4 collective-permute-start.7
  540.5 8.7 %copy-start.4 = (bf16[32,128,256]{2,1,0:T(8,128)(2,1)S(1)}, bf16[32,128,256]{2,1,0:T(8,128)(2,1)}, u32[]{:S(2)}) copy-start(bf16[32,128,256]{2,1,0:T(8,128)(2,1)} %get-tuple-element.3) | copy-start | bytes 6291460
  615.5 21.2 %copy-start.1 = (f32[1,32,128,256]{3,2,1,0:T(8,128)S(1)}, f32[1,32,128,256]{3,2,1,0:T(8,128)}, u32[]{:S(2)}) copy-start(f32[1,32,128,256]{3,2,1,0:T(8,128)} %fusion.74) | copy-start | bytes 12582916
  616.9 8.6 %collective-permute-start.8 = (f32[1,4,128,256]{3,2,1,0:T(8,128)S(1)}, f32[1,4,128,256]{3,2,1,0:T(8,128)S(1)}, u32[]{:S(2)}, u32[]{:S(2)}) collective-permute-start(f32[1,4,128,256]{3,2,1,0:T(8,128)S(1)} %get-tuple-element.24), channel_id=1, source_target_pairs={{2,0},{4,2},{6,4},{3,1},{5,3},{7,5},{10,8},{12,10},{14,12},{11,9},... | collective-permute-start | bytes 1572872 | tf_op jit(solution)/shard_map/ppermute | solution.py:25
  618.3 8.6 %collective-permute-start.9 = (f32[1,4,128,256]{3,2,1,0:T(8,128)S(1)}, f32[1,4,128,256]{3,2,1,0:T(8,128)S(1)}, u32[]{:S(2)}, u32[]{:S(2)}) collective-permute-start(f32[1,4,128,256]{3,2,1,0:T(8,128)S(1)} %get-tuple-element.25), channel_id=1, source_target_pairs={{0,2},{2,4},{4,6},{1,3},{3,5},{5,7},{8,10},{10,12},{12,14},{9,11},... | collective-permute-start | bytes 1572872 | tf_op jit(solution)/shard_map/ppermute | solution.py:22
  628.0 7.2 collective-permute-start.10
  629.3 7.4 collective-permute-start.11
  716.1 23.9 %copy-start.2 = (f32[1,32,128,256]{3,2,1,0:T(8,128)S(1)}, f32[1,32,128,256]{3,2,1,0:T(8,128)}, u32[]{:S(2)}) copy-start(f32[1,32,128,256]{3,2,1,0:T(8,128)} %fusion.43) | copy-start | bytes 12582916
  717.5 11.2 %collective-permute-start.12 = (f32[1,4,128,256]{3,2,1,0:T(8,128)S(1)}, f32[1,4,128,256]{3,2,1,0:T(8,128)S(1)}, u32[]{:S(2)}, u32[]{:S(2)}) collective-permute-start(f32[1,4,128,256]{3,2,1,0:T(8,128)S(1)} %get-tuple-element.22), channel_id=1, source_target_pairs={{2,0},{4,2},{6,4},{3,1},{5,3},{7,5},{10,8},{12,10},{14,12},{11,9},... | collective-permute-start | bytes 1572872 | tf_op jit(solution)/shard_map/ppermute | solution.py:25
  718.9 11.3 %collective-permute-start.13 = (f32[1,4,128,256]{3,2,1,0:T(8,128)S(1)}, f32[1,4,128,256]{3,2,1,0:T(8,128)S(1)}, u32[]{:S(2)}, u32[]{:S(2)}) collective-permute-start(f32[1,4,128,256]{3,2,1,0:T(8,128)S(1)} %get-tuple-element.23), channel_id=1, source_target_pairs={{0,2},{2,4},{4,6},{1,3},{3,5},{5,7},{8,10},{10,12},{12,14},{9,11},... | collective-permute-start | bytes 1572872 | tf_op jit(solution)/shard_map/ppermute | solution.py:22
  731.3 7.2 collective-permute-start.14
  732.6 7.4 collective-permute-start.15
  744.9 8.7 %copy-start.5 = (bf16[32,128,256]{2,1,0:T(8,128)(2,1)S(1)}, bf16[32,128,256]{2,1,0:T(8,128)(2,1)}, u32[]{:S(2)}) copy-start(bf16[32,128,256]{2,1,0:T(8,128)(2,1)} %get-tuple-element.5) | copy-start | bytes 6291460
Sparse Core Ops, SparseCore 0:
  33.4 432.1 all-reduce.6
where the time goes:
time: 835 us; the launch traced here: 826 us
  waiting for transfers between devices  418 us (50%)
  other arithmetic  312 us (37%)
  starting transfers between devices  52 us (6%)
  between operations  30.1 us (4%)
  local copies, waits for them, and re-layouts  14.6 us (2%)
    psum x1, waiting for transfers between devices, spread(): return lax.psum(kept, axis)  404 us
    sub x4, other arithmetic, shards(): 2.0 * current - previous + courant[None] * laplace - scaled * source[None]  253 us
    concatenate x10, other arithmetic, with_halo(): block = jnp.concatenate([low, block, high], axis=dim)  48.7 us
    ppermute x8, starting transfers between devices, with_halo(): lax.ppermute(lax.slice_in_dim(block, block.shape[dim] - width, None, axis...  41.4 us
  transfers between devices with their start and end apart: 17, of which 13 were waited for; matrix products, arithmetic and copies ran while one was open for 2% of the time, Pallas kernels for 0%

commit v1 on v0

v1 whole, which is shorter than its diff:
```python
import functools

import jax
import jax.numpy as jnp
import ml_dtypes
import numpy as np
from jax import lax
from jax.experimental import pallas as pl
from jax.experimental.pallas import tpu as pltpu
from jax.sharding import PartitionSpec as P

STEPS = 4
COEFFS = (-205.0 / 72.0, 8.0 / 5.0, -1.0 / 5.0, 8.0 / 315.0, -1.0 / 560.0)
W = 4
PAD = 16
NC = 4
MESH = pl.DeviceIdType.MESH


def band(rows, cols, shift):
    out = np.zeros((rows, cols), np.float64)
    for r in range(rows):
        for k in range(1, 5):
            for c in (r + shift - k, r + shift + k):
                if 0 <= c < cols:
                    out[r, c] += COEFFS[k]
    return out


def halves(matrix):
    high = matrix.astype(ml_dtypes.bfloat16)
    low = (matrix - high.astype(np.float64)).astype(ml_dtypes.bfloat16)
    return high, low


def kernel(
    n_probe,
    n_gx,
    n_gy,
    slots,
    precond,
    ids,
    ymat,
    zmat,
    prev_hbm,
    cur_hbm,
    cou_hbm,
    per_hbm,
    snap_hbm,
    early_hbm,
    late_hbm,
    field,
    cou,
    per,
    own,
    up,
    down,
    frames,
    load_sem,
    out_sem,
    up_send,
    up_recv,
    down_send,
    down_recv,
    halo_send,
    halo_recv,
):
    z = lax.axis_index("probe")
    gx = lax.axis_index("gx")
    gy = lax.axis_index("gy")
    nx, ny = cou.shape[0], cou.shape[1]
    ch = nx // NC
    slot_dev = own.shape[0]
    n_snap = slots.shape[0]
    last_slot = n_probe * slot_dev - 1
    total = (n_snap - 1) * NC
    body_x = pl.ds(W, nx)
    body_y = pl.ds(PAD, ny)

    loads = [
        pltpu.make_async_copy(snap_hbm, own, load_sem.at[0]),
        pltpu.make_async_copy(cur_hbm.at[0], field.at[0, body_x, body_y], load_sem.at[1]),
        pltpu.make_async_copy(prev_hbm.at[0], field.at[1, body_x, body_y], load_sem.at[2]),
        pltpu.make_async_copy(cou_hbm, cou, load_sem.at[3]),
        pltpu.make_async_copy(per_hbm.at[0], per, load_sem.at[4]),
    ]
    for load in loads:
        load.start()

    nz = cou.shape[2]
    zero_plane = jnp.zeros((ny, nz), jnp.float32)
    zero_rows = jnp.zeros((PAD, nz), jnp.float32)
    for b in range(2):
        for x in range(W):
            field[b, x, body_y] = zero_plane
            field[b, W + nx + x, body_y] = zero_plane

        def clear(x, carry, b=b):
            field[b, W + x, pl.ds(0, PAD)] = zero_rows
            field[b, W + x, pl.ds(PAD + ny, PAD)] = zero_rows
            return carry

        lax.fori_loop(0, nx, clear, 0)

    sides = (
        (z < n_probe - 1, {"probe": z + 1}),
        (z > 0, {"probe": z - 1}),
        (gx < n_gx - 1, {"gx": gx + 1}),
        (gx > 0, {"gx": gx - 1}),
        (gy < n_gy - 1, {"gy": gy + 1}),
        (gy > 0, {"gy": gy - 1}),
    )
    barrier = pltpu.get_barrier_semaphore()
    for there, target in sides:

        @pl.when(there)
        def _():
            pl.semaphore_signal(barrier, inc=1, device_id=target, device_id_type=MESH)

    pl.semaphore_wait(barrier, sum(there.astype(jnp.int32) for there, _ in sides))

    halo_out = (
        (pl.ds(nx, W), body_y, pl.ds(0, W), body_y),
        (pl.ds(W, W), body_y, pl.ds(W + nx, W), body_y),
        (body_x, pl.ds(PAD + ny - 8, 8), body_x, pl.ds(PAD - 8, 8)),
        (body_x, pl.ds(PAD, 8), body_x, pl.ds(PAD + ny, 8)),
    )
    back = (1, 0, 3, 2)

    def halo(e, side):
        sx, sy, dx, dy = halo_out[side]
        return pltpu.make_async_remote_copy(
            src_ref=field.at[e % 2, sx, sy],
            dst_ref=field.at[e % 2, dx, dy],
            send_sem=halo_send.at[e, side],
            recv_sem=halo_recv.at[e, side],
            device_id=sides[2 + side][1],
            device_id_type=MESH,
        )

    def halo_start(e):
        for side in range(4):

            @pl.when(sides[2 + side][0])
            def _():
                halo(e, side).start()

    def halo_wait(e):
        for side in range(4):

            @pl.when(sides[2 + side][0])
            def _():
                halo(e, side).wait_send()
                halo(e, back[side]).wait_recv()

    at = [slots[j] for j in range(n_snap)]
    owner = [lax.div(a, slot_dev) for a in at]
    first_pos = jnp.int32(0)
    last_pos = jnp.int32(0)
    for j in range(n_snap):
        first_pos = jnp.where(at[j] == 0, j, first_pos)
        last_pos = jnp.where(at[j] == last_slot, j, last_pos)

    def relay(k, buf, skipped, at_source, forwards, target, send, recv):
        def link(i):
            return pltpu.make_async_remote_copy(
                src_ref=buf.at[i],
                dst_ref=buf.at[i],
                send_sem=send.at[i],
                recv_sem=recv.at[i],
                device_id=target,
                device_id_type=MESH,
            )

        @pl.when((k >= 0) & (k < total))
        def _():
            m = lax.div(k, NC)
            c = k - m * NC
            position = m + jnp.where(m >= skipped, 1, 0)
            slot = slots[position]
            mine = lax.div(slot, slot_dev) == z
            which = lax.rem(slot, slot_dev)

            @pl.when(at_source)
            def _():
                def fill(i, carry):
                    buf[k, i] = own[which, c * ch + i]
                    return carry

                lax.fori_loop(0, ch, fill, 0)

            @pl.when(jnp.logical_not(at_source))
            def _():
                link(k).wait_recv()

                def fill(i, carry):
                    buf[k, i] = lax.select(mine, own[which, c * ch + i], buf[k, i])
                    return carry

                lax.fori_loop(0, ch, fill, 0)

            @pl.when(forwards)
            def _():
                link(k).start()

        return link

    def comm(s):
        relay(s - z, up, last_pos, z == 0, z < n_probe - 1, {"probe": z + 1}, up_send, up_recv)
        relay(
            s - (n_probe - 1 - z),
            down,
            first_pos,
            z == n_probe - 1,
            z > 0,
            {"probe": z - 1},
            down_send,
            down_recv,
        )

    def snapshot(j, c, i):
        def pick(buf, skipped):
            if j == 0:
                return buf[c, i]
            before = buf[(j - 1) * NC + c, i]
            if j == n_snap - 1:
                return before
            return lax.select(skipped < j, before, buf[j * NC + c, i])

        from_up = (owner[j] <= z) & (last_pos != j)
        return lax.select(from_up, pick(up, last_pos), pick(down, first_pos))

    weight = precond[ids[0]]

    def plane(n, c, i):
        a, b = n % 2, 1 - n % 2
        x = c * ch + i
        if n == 0:
            frames[0, x] = snapshot(0, c, i)
            frames[1, x] = snapshot(1, c, i)
        newest = snapshot(n + 2, c, i)
        if n < STEPS - 1:
            frames[(n + 2) % 3, x] = newest
        source = (
            newest.astype(jnp.float32)
            - 2.0 * frames[(n + 1) % 3, x].astype(jnp.float32)
            + frames[n % 3, x].astype(jnp.float32)
        )
        padded = field[a, x + W]
        high = padded.astype(jnp.bfloat16)
        low = (padded - high.astype(jnp.float32)).astype(jnp.bfloat16)
        lap = jnp.dot(
            ymat[...],
            jnp.concatenate([high, low, high], axis=0),
            preferred_element_type=jnp.float32,
        )
        high = high[PAD : PAD + ny]
        low = low[PAD : PAD + ny]
        lap = lap + jnp.dot(
            jnp.concatenate([high, low, high], axis=1),
            zmat[...],
            preferred_element_type=jnp.float32,
        )
        here = field[a, x + W, body_y]
        lap = lap + (3.0 * COEFFS[0]) * here
        for k in range(1, 5):
            lap = lap + COEFFS[k] * (field[a, x + W + k, body_y] + field[a, x + W - k, body_y])
        field[b, x + W, body_y] = (
            2.0 * here - field[b, x + W, body_y] + cou[x] * lap - (weight * per[x]) * source
        )

    for load in loads[:2]:
        load.wait()
    halo_start(0)

    def lead(s, carry):
        comm(s)
        return carry

    start = 2 * NC + n_probe - 1
    lax.fori_loop(0, start, lead, 0)
    for load in loads[2:]:
        load.wait()

    early = pltpu.make_async_copy(field.at[1, body_x, body_y], early_hbm.at[0], out_sem.at[NC])

    def late(c):
        return pltpu.make_async_copy(
            field.at[0, pl.ds(W + c * ch, ch), body_y],
            late_hbm.at[0, pl.ds(c * ch, ch)],
            out_sem.at[c],
        )

    for n in range(STEPS):
        def chunk(c, carry, n=n):
            if n < STEPS - 1:
                comm(start + NC * n + c)

            def planes(i, carry):
                plane(n, c, i)
                return carry

            lax.fori_loop(0, ch, planes, 0)
            if n == STEPS - 1:
                late(c).start()
            return carry

        halo_wait(n)
        if n == STEPS - 1:
            early.start()
        lax.fori_loop(0, NC, chunk, 0)
        if n < STEPS - 1:
            halo_start(n + 1)

    def finish(k, carry):
        @pl.when(z < n_probe - 1)
        def _():
            relay_link(up, up_send, up_recv, {"probe": z + 1}, k).wait_send()

        @pl.when(z > 0)
        def _():
            relay_link(down, down_send, down_recv, {"probe": z - 1}, k).wait_send()

        return carry

    lax.fori_loop(0, total, finish, 0)
    early.wait()

    def flush(c, carry):
        late(c).wait()
        return carry

    lax.fori_loop(0, NC, flush, 0)


def relay_link(buf, send, recv, target, i):
    return pltpu.make_async_remote_copy(
        src_ref=buf.at[i],
        dst_ref=buf.at[i],
        send_sem=send.at[i],
        recv_sem=recv.at[i],
        device_id=target,
        device_id_type=MESH,
    )


def shards(sizes, wave_prev, wave_cur, courant, perturb, snapshots, step_slots, precond, probe_ids):
    nx, ny, nz = courant.shape
    slot_dev = snapshots.shape[0]
    total = (step_slots.shape[0] - 1) * NC
    y_high, y_low = halves(band(ny, ny + 2 * PAD, PAD))
    z_high, z_low = halves(band(nz, nz, 0))
    ymat = jnp.asarray(np.concatenate([y_high, y_high, y_low], axis=1))
    zmat = jnp.asarray(np.concatenate([z_high, z_high, z_low], axis=0))
    smem = pl.BlockSpec(memory_space=pltpu.SMEM)
    vmem = pl.BlockSpec(memory_space=pltpu.VMEM)
    hbm = pl.BlockSpec(memory_space=pl.ANY)
    wave = jax.ShapeDtypeStruct(wave_cur.shape, jnp.float32)
    dma = pltpu.SemaphoreType.DMA
    messages = pltpu.VMEM((total, nx // NC, ny, nz), jnp.bfloat16)
    return pl.pallas_call(
        functools.partial(kernel, *sizes),
        out_shape=(wave, wave),
        in_specs=[smem, smem, smem, vmem, vmem] + [hbm] * 5,
        out_specs=(hbm, hbm),
        scratch_shapes=[
            pltpu.VMEM((2, nx + 2 * W, ny + 2 * PAD, nz), jnp.float32),
            pltpu.VMEM((nx, ny, nz), jnp.float32),
            pltpu.VMEM((nx, ny, nz), jnp.float32),
            pltpu.VMEM((slot_dev, nx, ny, nz), jnp.bfloat16),
            messages,
            messages,
            pltpu.VMEM((3, nx, ny, nz), jnp.bfloat16),
            dma((5,)),
            dma((NC + 1,)),
            dma((total,)),
            dma((total,)),
            dma((total,)),
            dma((total,)),
            dma((STEPS, 4)),
            dma((STEPS, 4)),
        ],
        compiler_params=pltpu.CompilerParams(
            collective_id=0, has_side_effects=True, vmem_limit_bytes=60 * 1024 * 1024
        ),
    )(
        step_slots,
        precond,
        probe_ids,
        ymat,
        zmat,
        wave_prev,
        wave_cur,
        courant,
        perturb,
        snapshots,
    )


def solution(mesh):
    placed = (
        P("probe", "gx", "gy", None),
        P("probe", "gx", "gy", None),
        P("gx", "gy", None),
        P("probe", "gx", "gy", None),
        P("probe", "gx", "gy", None),
        P(),
        P(),
        P("probe"),
    )
    sizes = (mesh.shape["probe"], mesh.shape["gx"], mesh.shape["gy"])
    return jax.shard_map(
        functools.partial(shards, sizes),
        mesh=mesh,
        in_specs=placed,
        out_specs=(P("probe", "gx", "gy", None), P("probe", "gx", "gy", None)),
        check_vma=False,
    )
```

time: 835 us -> 297 us (0.36); the launches traced: 826 us -> 297 us
  waiting for transfers between devices: 418 us -> 0 us
  other arithmetic: 312 us -> 0 us
  Pallas kernels: 0 us -> 289 us
  starting transfers between devices: 52 us -> 0 us
  between operations: 30.1 us -> 1.3 us
    psum x1 -> x0, waiting for transfers between devices: 404 us -> none  [spread(): return lax.psum(kept, axis)]
    pallas_call x0 -> x1, Pallas kernels: none -> 289 us  [shards(): pl.pallas_call(functools.partial(kernel, *sizes), out_shape=(wave, wave),...]
    sub x4 -> x0, other arithmetic: 253 us -> none  [shards(): 2.0 * current - previous + courant[None] * laplace - scaled * source[None]]
    ppermute x16 -> x0, starting transfers between devices: 52 us -> none  [the longest x8 41.4 us: with_halo(): lax.ppermute(lax.slice_in_dim(block, block.shape[dim] - width, None, axis...]
    concatenate x10 -> x0, other arithmetic: 48.7 us -> none  [with_halo(): block = jnp.concatenate([low, block, high], axis=dim)]
    ppermute x16 -> x0, waiting for transfers between devices: 13.9 us -> none  [the longest x8 10.5 us: with_halo(): lax.ppermute(lax.slice_in_dim(block, block.shape[dim] - width, None, axis...]
    select_n x1 -> x0, other arithmetic: 9.39 us -> none  [spread(): jnp.where(lax.axis_index(axis) == source, value, 0).astype(value.dtype)]
  transfers between devices with their start and end apart: 17 -> 0, of which waited for: 13 -> 0; matrix products, arithmetic and copies ran while one was open for 2% -> 0% of each run, Pallas kernels for 0% -> 0%
where the time goes in v1:
time: 297 us
  Pallas kernels  289 us (97%)
  local copies, waits for them, and re-layouts  6.82 us (2%)
    pallas_call x1, Pallas kernels, shards(): pl.pallas_call(functools.partial(kernel, *sizes), out_shape=(wave, wave),...  289 us
    unnamed x4, local copies, waits for them, and re-layouts  6.82 us

profile of v1, /device:TPU:0, one launch (start us, length us, event | category | flops | bytes accessed | tf_op | source)
XLA Modules:
  0.0 296.8 jit_solution(14555265651786274515)
XLA Ops:
  1.3 288.7 %shard_map.113 = (f32[1,32,128,256]{3,2,1,0:T(8,128)}, f32[1,32,128,256]{3,2,1,0:T(8,128)}) custom-call(s32[6]{0:T(128)} %slots.1, f32[256]{0:T(256)} %precond.1, s32[1]{0:T(128)S(6)} %copy.14.ids, bf16[128,480]{1,0:T(8,128)(2,1)} %constant.4.clone.ymat, bf16[768,256]{1,0:T(8,128)(2,1)} %constant.5.clone.zmat, f32[1,32,128,256]{3,2,1,0:T(8,128)} %prev_hbm.1, ...), custom_call_target="tpu_custom_call" | custom-call | tf_op jit(solution)/shard_map/pallas_call | solution.py:361
  289.9 0.0 copy-start
  290.0 4.8 %copy.15 = f32[1,32,128,256]{3,2,1,0:T(8,128)} copy(f32[1,32,128,256]{3,2,1,0:T(8,128)} %get-tuple-element.4) | data formatting | bytes 8388608
  294.8 0.0 copy-done
  294.8 2.0 copy.16
Async XLA Ops:
  289.9 4.8 %copy-start = (f32[1,32,128,256]{3,2,1,0:T(8,128)S(1)}, f32[1,32,128,256]{3,2,1,0:T(8,128)}, u32[]{:S(2)}) copy-start(f32[1,32,128,256]{3,2,1,0:T(8,128)} %get-tuple-element.5) | copy-start | bytes 12582916

commit v2 on v1

--- a/solution.py
+++ b/solution.py
@@ -13,7 +13,8 @@
 COEFFS = (-205.0 / 72.0, 8.0 / 5.0, -1.0 / 5.0, 8.0 / 315.0, -1.0 / 560.0)
 W = 4
 PAD = 16
-NC = 4
+NC = 8
+LAG = 2
 MESH = pl.DeviceIdType.MESH
 
 
@@ -206,9 +207,9 @@
         return link
 
     def comm(s):
-        relay(s - z, up, last_pos, z == 0, z < n_probe - 1, {"probe": z + 1}, up_send, up_recv)
+        relay(s - LAG * z, up, last_pos, z == 0, z < n_probe - 1, {"probe": z + 1}, up_send, up_recv)
         relay(
-            s - (n_probe - 1 - z),
+            s - LAG * (n_probe - 1 - z),
             down,
             first_pos,
             z == n_probe - 1,
@@ -277,7 +278,7 @@
         comm(s)
         return carry
 
-    start = 2 * NC + n_probe - 1
+    start = 2 * NC + LAG * (n_probe - 1)
     lax.fori_loop(0, start, lead, 0)
     for load in loads[2:]:
         load.wait()

time: 297 us -> 286 us (0.963)
  Pallas kernels: 289 us -> 277 us
    pallas_call x1, Pallas kernels: 289 us -> 277 us  [shards(): pl.pallas_call(functools.partial(kernel, *sizes), out_shape=(wave, wave),...]
where the time goes in v2:
time: 286 us
  Pallas kernels  277 us (97%)
  local copies, waits for them, and re-layouts  6.82 us (2%)
    pallas_call x1, Pallas kernels, shards(): pl.pallas_call(functools.partial(kernel, *sizes), out_shape=(wave, wave),...  277 us
    unnamed x4, local copies, waits for them, and re-layouts  6.82 us

profile of v2, /device:TPU:0, one launch (start us, length us, event | category | flops | bytes accessed | tf_op | source)
XLA Modules:
  0.0 285.5 jit_solution(5006688769412978039)
XLA Ops:
  1.3 277.4 %shard_map.113 = (f32[1,32,128,256]{3,2,1,0:T(8,128)}, f32[1,32,128,256]{3,2,1,0:T(8,128)}) custom-call(s32[6]{0:T(128)} %slots.1, f32[256]{0:T(256)} %precond.1, s32[1]{0:T(128)S(6)} %copy.14.ids, bf16[128,480]{1,0:T(8,128)(2,1)} %constant.4.clone.ymat, bf16[768,256]{1,0:T(8,128)(2,1)} %constant.5.clone.zmat, f32[1,32,128,256]{3,2,1,0:T(8,128)} %prev_hbm.1, ...), custom_call_target="tpu_custom_call" | custom-call | tf_op jit(solution)/shard_map/pallas_call | solution.py:362
  278.7 0.0 copy-start
  278.7 4.8 %copy.15 = f32[1,32,128,256]{3,2,1,0:T(8,128)} copy(f32[1,32,128,256]{3,2,1,0:T(8,128)} %get-tuple-element.4) | data formatting | bytes 8388608
  283.5 0.0 copy-done
  283.5 2.0 copy.16
Async XLA Ops:
  278.7 4.8 %copy-start = (f32[1,32,128,256]{3,2,1,0:T(8,128)S(1)}, f32[1,32,128,256]{3,2,1,0:T(8,128)}, u32[]{:S(2)}) copy-start(f32[1,32,128,256]{3,2,1,0:T(8,128)} %get-tuple-element.5) | copy-start | bytes 12582916

commit v3 on v2

--- a/solution.py
+++ b/solution.py
@@ -13,8 +13,8 @@
 COEFFS = (-205.0 / 72.0, 8.0 / 5.0, -1.0 / 5.0, 8.0 / 315.0, -1.0 / 560.0)
 W = 4
 PAD = 16
-NC = 8
-LAG = 2
+NC = 16
+LAG = 3
 MESH = pl.DeviceIdType.MESH
 
 

time: 286 us -> 282 us (0.986); the launches traced: 286 us -> 277 us
  Pallas kernels: 277 us -> 269 us
    pallas_call x1, Pallas kernels: 277 us -> 269 us  [shards(): pl.pallas_call(functools.partial(kernel, *sizes), out_shape=(wave, wave),...]
where the time goes in v3:
time: 282 us; the launch traced here: 277 us
  Pallas kernels  269 us (95%)
  local copies, waits for them, and re-layouts  6.82 us (2%)
    pallas_call x1, Pallas kernels, shards(): pl.pallas_call(functools.partial(kernel, *sizes), out_shape=(wave, wave),...  269 us
    unnamed x4, local copies, waits for them, and re-layouts  6.82 us

profile of v3, /device:TPU:0, one launch (start us, length us, event | category | flops | bytes accessed | tf_op | source)
XLA Modules:
  0.0 277.3 jit_solution(10718981427639131483)
XLA Ops:
  1.3 269.2 %shard_map.113 = (f32[1,32,128,256]{3,2,1,0:T(8,128)}, f32[1,32,128,256]{3,2,1,0:T(8,128)}) custom-call(s32[6]{0:T(128)} %slots.1, f32[256]{0:T(256)} %precond.1, s32[1]{0:T(128)S(6)} %copy.14.ids, bf16[128,480]{1,0:T(8,128)(2,1)} %constant.4.clone.ymat, bf16[768,256]{1,0:T(8,128)(2,1)} %constant.5.clone.zmat, f32[1,32,128,256]{3,2,1,0:T(8,128)} %prev_hbm.1, ...), custom_call_target="tpu_custom_call" | custom-call | tf_op jit(solution)/shard_map/pallas_call | solution.py:362
  270.4 0.0 copy-start
  270.5 4.8 %copy.15 = f32[1,32,128,256]{3,2,1,0:T(8,128)} copy(f32[1,32,128,256]{3,2,1,0:T(8,128)} %get-tuple-element.4) | data formatting | bytes 8388608
  275.3 0.0 copy-done
  275.3 2.0 copy.16
Async XLA Ops:
  270.4 4.8 %copy-start = (f32[1,32,128,256]{3,2,1,0:T(8,128)S(1)}, f32[1,32,128,256]{3,2,1,0:T(8,128)}, u32[]{:S(2)}) copy-start(f32[1,32,128,256]{3,2,1,0:T(8,128)} %get-tuple-element.5) | copy-start | bytes 12582916
